TPU v7x, 32 devices: a whole 2x2x4 slice. The times are simulated.
32 devices in a mesh: section: 8 (over y, x, core), dp: 4 (over z).
Axes of the slice: x: 2, y: 2, z: 4, core: 2. Of those that a mesh axis runs over, the one named last changes fastest.
Arguments:
- inputs: bfloat16 [4, 8, 128, 4096], P('dp', 'section'), may hold values from -6 to 6
- key_rows: bfloat16 [4, 8, 24, 4096], P('dp', None, None, 'section'), may hold values from -32 to 32
- value_rows: bfloat16 [4, 8, 24, 4096], P('dp', None, None, 'section'), may hold values from -6 to 6
- query_gain: float32 [8, 4096], P('section'), may hold values from 0.1 to 1.9
- cotangent: bfloat16 [4, 8, 128, 4096], P('dp', 'section'), may hold values from -6 to 6
Outputs:
- key_grads: bfloat16 [4, 8, 24, 4096], P('dp', None, None, 'section')
- value_grads: bfloat16 [4, 8, 24, 4096], P('dp', None, None, 'section')
- gain_grads: float32 [8, 4096], P('section')
All inputs are finite; a program needn't handle non-finite values.
Results may differ from a plain program's by a relative error of at most 0.008.
Values may be sent and summed in bfloat16 or wider, within the bound.
A program may use at most 64 MiB of HBM per device.

v0:
```python
import functools

import jax
import jax.numpy as jnp
from jax import lax
from jax.experimental import pallas as pl
from jax.experimental.pallas import tpu as pltpu
from jax.sharding import PartitionSpec as P

HEAD = 64
TICKS = 3
LANES = 128
MESH = pl.DeviceIdType.MESH
F32 = jnp.float32
BF16 = jnp.bfloat16


def nn(a, b):
    return lax.dot_general(a, b, (((1,), (0,)), ((), ())), preferred_element_type=F32)


def nt(a, b):
    return lax.dot_general(a, b, (((1,), (1,)), ((), ())), preferred_element_type=F32)


def kernel(
    n, ndp, unroll,
    x_ref, ct_ref, k_ref, v_ref, g_ref,
    kout_ref, vout_ref, gout_ref,
    xin, cin, gin, stat, kd, vd, kdt, vdt, gt, xs, qs, probs, plow, raws, ds, grads,
    red, inv, ar, ktot, vtot, gsend, gdp,
    x_send, x_recv, c_send, c_recv, g_send, g_recv, st_send, st_recv,
    ar_send, ar_recv, dp_send, dp_recv, loc,
):
    me = lax.axis_index("section")
    doc = lax.axis_index("dp")
    tok, width = x_ref.shape
    src, cols = k_ref.shape[1], k_ref.shape[2]
    blocks = cols // LANES
    per = LANES // HEAD
    brow = per * src
    scale = HEAD ** (-0.5)

    def peers(body, first=1, last=n):
        def step(j, c):
            body(lax.rem(me + j, n))
            return c
        lax.fori_loop(first, last, step, 0)

    def each(body, first=0, last=n, u=None):
        def step(m, c):
            body(m)
            return c
        lax.fori_loop(first, last, step, 0, unroll=u or min(unroll, last - first))

    half = n // 2
    halves = ((0, half), (half, n))

    def to(p, source, target, send, recv):
        return pltpu.make_async_remote_copy(
            src_ref=source, dst_ref=target, send_sem=send, recv_sem=recv,
            device_id={"section": p}, device_id_type=MESH)

    def others(body):
        def step(j, c):
            place = lax.rem(doc * n + me + j, n * ndp)
            body(lax.div(place, n), lax.rem(place, n))
            return c
        lax.fori_loop(1, n * ndp, step, 0)

    def cut(ref, p):
        return ref.at[:, pl.ds(pl.multiple_of(p * cols, LANES), cols)]

    def x_copy(p, slot):
        return to(p, cut(x_ref, p), xin.at[slot], x_send.at[p], x_recv.at[slot])

    def c_copy(p, slot):
        return to(p, cut(ct_ref, p), cin.at[slot], c_send.at[p], c_recv.at[slot])

    def g_copy(p, slot):
        return to(p, cut(g_ref, p), gin.at[slot], g_send.at[p], g_recv.at[slot])

    def st_copy(p, slot):
        return to(p, stat.at[me], stat.at[slot], st_send.at[p], st_recv.at[slot])

    def ar_copy(a, h, p, slot):
        lo, hi = halves[h]
        return to(p, ar.at[a, me, lo:hi], ar.at[a, slot, lo:hi], ar_send.at[a, h, p], ar_recv.at[a, h, slot])

    def share(a, h):
        peers(lambda p: ar_copy(a, h, p, me).start())

    def dp_copy(q, p, from_doc, slot):
        return pltpu.make_async_remote_copy(
            src_ref=gsend.at[p], dst_ref=gdp.at[from_doc, slot],
            send_sem=dp_send.at[q, p], recv_sem=dp_recv.at[from_doc, slot],
            device_id={"dp": q, "section": p}, device_id_type=MESH)

    barrier = pltpu.get_barrier_semaphore()
    others(lambda q, p: pl.semaphore_signal(
        barrier, inc=1, device_id={"dp": q, "section": p}, device_id_type=MESH))

    total = jnp.zeros((tok, LANES), F32)
    for b in range(width // LANES):
        part = x_ref[:, b * LANES:(b + 1) * LANES].astype(F32)
        total = total + part * part
    stat[me] = jnp.sum(total.T, axis=0, keepdims=True)

    pl.semaphore_wait(barrier, n * ndp - 1)

    peers(lambda p: g_copy(p, me).start())
    peers(lambda p: st_copy(p, me).start())
    peers(lambda p: x_copy(p, me).start())
    first_cut, second_cut = (1 + n) // 4, 1 + (5 * n) // 8
    peers(lambda p: c_copy(p, me).start(), 1, first_cut)
    own = [
        pltpu.make_async_copy(cut(g_ref, me), gin.at[me], loc.at[0]),
        pltpu.make_async_copy(cut(x_ref, me), xin.at[me], loc.at[1]),
        pltpu.make_async_copy(cut(ct_ref, me), cin.at[me], loc.at[2]),
    ]
    for copy in own:
        copy.start()

    lane = lax.broadcasted_iota(jnp.int32, (src, LANES), 1)
    sides = [jnp.logical_and(lane >= i * HEAD, lane < (i + 1) * HEAD) for i in range(per)]

    def spread(l):
        for source, plain, turned in ((k_ref, kd, kdt), (v_ref, vd, vdt)):
            rows = source[l].astype(F32)
            for b in range(blocks):
                piece = rows[:, b * LANES:(b + 1) * LANES]
                both = jnp.concatenate([jnp.where(s, piece, 0.0) for s in sides], axis=0)
                plain[l, b] = both.astype(BF16)
                turned[l, b] = both.T.astype(BF16)
        ktot[l] = jnp.zeros((src, cols), F32)
        vtot[l] = jnp.zeros((src, cols), F32)

    each(spread, u=2)

    own[0].wait()
    peers(lambda p: g_copy(p, p).wait_recv())

    def turn_gain(l):
        for b in range(blocks):
            row = gin[l, :, b * LANES:(b + 1) * LANES]
            gt[l, b * LANES:(b + 1) * LANES, :] = jnp.broadcast_to(row, (LANES, LANES)).T

    each(turn_gain, u=2)
    peers(lambda p: st_copy(p, p).wait_recv())

    def fwd(k, m, more):
        l = lax.rem(m + k, n)
        factor = inv[k, m]
        pieces = []
        sums = jnp.zeros((1, tok), F32)
        for b in range(blocks):
            at = slice(b * LANES, (b + 1) * LANES)
            rows = slice(b * brow, (b + 1) * brow)
            xf = xs[k, m, at, :].astype(F32)
            q = (xf * factor * gt[l, at, :]).astype(BF16)
            qs[k, m, at, :] = q
            raw = nn(kd[l, b], q)
            raws[k, m, rows, :] = raw
            s3 = raw.reshape(per, src, tok) * scale
            w = jnp.exp(s3 - jnp.max(s3, axis=1, keepdims=True))
            p = w * (1.0 / jnp.sum(w, axis=1, keepdims=True))
            p = p.reshape(brow, tok)
            probs[k, m, rows, :] = p
            low = p.astype(BF16)
            plow[k, m, rows, :] = low
            if more:
                y = (xf + nn(vdt[l, b], low)).astype(BF16)
                xs[k + 1, m, at, :] = y
                yf = y.astype(F32)
                sums = sums + jnp.sum(yf * yf, axis=0, keepdims=True)
        if more:
            ar[k, me, m] = sums

    def reduced(a, h):
        lo, hi = halves[h]
        peers(lambda p: ar_copy(a, h, p, p).wait_recv())
        total = ar[a, 0, lo:hi]
        for s in range(1, n):
            total = total + ar[a, s, lo:hi]
        return total * (1.0 / width)

    def arrive(j, c):
        m = lax.rem(me + j, n)

        @pl.when(j == 0)
        def _():
            own[1].wait()

        @pl.when(j > 0)
        def _():
            x_copy(m, m).wait_recv()

        inv[0, m] = lax.rsqrt(stat[m] * (1.0 / width) + 1e-6)
        for b in range(blocks):
            at = slice(b * LANES, (b + 1) * LANES)
            xs[0, m, at, :] = xin[m, :, at].T
        fwd(0, m, True)
        return c

    lax.fori_loop(0, n, arrive, 0)
    share(0, 0)
    share(0, 1)
    peers(lambda p: c_copy(p, me).start(), first_cut, second_cut)
    for k in range(1, TICKS):
        for h, (lo, hi) in enumerate(halves):
            inv[k, lo:hi] = lax.rsqrt(reduced(k - 1, h) + 1e-6)
            each(lambda m: fwd(k, m, k + 1 < TICKS), lo, hi)
            if k + 1 < TICKS:
                share(k, h)
        if k == 1:
            peers(lambda p: c_copy(p, me).start(), second_cut, n)

    own[2].wait()

    def arrive_c(p):
        c_copy(p, p).wait_recv()

    def turn_c(m):
        s = lax.rem(m + TICKS, n)
        for b in range(blocks):
            at = slice(b * LANES, (b + 1) * LANES)
            grads[TICKS - 1, m, at, :] = cin[s, :, at].T

    peers(arrive_c)

    def scores_back(k, a, m):
        l = lax.rem(m + k, n)
        sums = jnp.zeros((1, tok), F32)
        for b in range(blocks):
            at = slice(b * LANES, (b + 1) * LANES)
            rows = slice(b * brow, (b + 1) * brow)
            dprob = nn(vd[l, b], grads[k, m, at, :]).reshape(per, src, tok)
            p = probs[k, m, rows, :].reshape(per, src, tok)
            mean = jnp.sum(p * dprob, axis=1, keepdims=True)
            d = (p * (dprob - mean) * scale).reshape(brow, tok).astype(BF16)
            ds[k, m, rows, :] = d
            if a is not None:
                sums = sums + jnp.sum(d.astype(F32) * raws[k, m, rows, :], axis=0, keepdims=True)
        if a is not None:
            ar[a, me, m] = sums

    def picked(r):
        out = r[:src]
        for i in range(1, per):
            out = jnp.where(sides[i], r[i * src:(i + 1) * src], out)
        return out

    def key_step(k, m):
        l = lax.rem(m + k, n)
        for b in range(blocks):
            at = slice(b * LANES, (b + 1) * LANES)
            rows = slice(b * brow, (b + 1) * brow)
            ktot[l, :, at] += picked(nt(ds[k, m, rows, :], qs[k, m, at, :]))

    def value_step(k, m):
        l = lax.rem(m + k, n)
        for b in range(blocks):
            at = slice(b * LANES, (b + 1) * LANES)
            rows = slice(b * brow, (b + 1) * brow)
            vtot[l, :, at] += picked(nt(plow[k, m, rows, :], grads[k, m, at, :]))

    def input_back(k, m):
        l = lax.rem(m + k, n)
        factor = inv[k, m]
        mean = red[m]
        for b in range(blocks):
            at = slice(b * LANES, (b + 1) * LANES)
            rows = slice(b * brow, (b + 1) * brow)
            dq = nn(kdt[l, b], ds[k, m, rows, :])
            u = xs[k, m, at, :].astype(F32) * factor
            back = grads[k, m, at, :].astype(F32) + factor * (gt[l, at, :] * dq - u * mean)
            grads[k - 1, m, at, :] = back.astype(BF16)

    def start_back(m):
        turn_c(m)
        scores_back(TICKS - 1, 2 * TICKS - 3, m)

    for h, (lo, hi) in enumerate(halves):
        each(start_back, lo, hi)
        share(2 * TICKS - 3, h)
    for k in range(TICKS - 1, 0, -1):
        a = TICKS - 1 + k - 1

        def next_back(m):
            input_back(k, m)
            scores_back(k - 1, a - 1 if k > 1 else None, m)

        each(lambda m: key_step(k, m))
        for h, (lo, hi) in enumerate(halves):
            red[lo:hi] = reduced(a, h)
            each(next_back, lo, hi)
            if k > 1:
                share(a - 1, h)

    def last(m):
        key_step(0, m)
        steps = ktot[m]
        kout_ref[m] = steps.astype(BF16)
        gsend[m] = jnp.sum(steps * k_ref[m].astype(F32), axis=0, keepdims=True) / gin[m]

    each(last)
    others(lambda q, p: dp_copy(q, p, doc, me).start())
    gdp[doc, me] = gsend[me]

    each(lambda m: value_step(TICKS - 1, m))
    for k in range(1, TICKS - 1):
        each(lambda m: value_step(k, m))

    def finish(m):
        value_step(0, m)
        vout_ref[m] = vtot[m].astype(BF16)

    each(finish)

    def drain(p):
        x_copy(p, me).wait_send()
        c_copy(p, me).wait_send()
        g_copy(p, me).wait_send()
        st_copy(p, me).wait_send()
        for a in range(2 * (TICKS - 1)):
            for h in range(2):
                ar_copy(a, h, p, me).wait_send()

    peers(drain)
    others(lambda q, p: dp_copy(q, p, q, p).wait_recv())
    others(lambda q, p: dp_copy(q, p, doc, me).wait_send())
    for s in range(n):
        out = gdp[0, s]
        for d in range(1, ndp):
            out = out + gdp[d, s]
        gout_ref[:, s * cols:(s + 1) * cols] = out


def on_device(inputs, key_rows, value_rows, query_gain, cotangent):
    n = lax.axis_size("section")
    ndp = lax.axis_size("dp")
    tok, width = inputs.shape[2:]
    src, cols = key_rows.shape[2:]
    blocks = cols // LANES
    brow = LANES // HEAD * src
    rows = blocks * brow
    rounds = 2 * (TICKS - 1)
    vmem = pltpu.VMEM
    sem = pltpu.SemaphoreType.DMA
    scratch = [
        vmem((n, tok, cols), BF16), vmem((n, tok, cols), BF16),
        vmem((n, 1, cols), F32), vmem((n, 1, tok), F32),
        vmem((n, blocks, brow, LANES), BF16), vmem((n, blocks, brow, LANES), BF16),
        vmem((n, blocks, LANES, brow), BF16), vmem((n, blocks, LANES, brow), BF16),
        vmem((n, cols, LANES), F32),
        vmem((TICKS, n, cols, tok), BF16), vmem((TICKS, n, cols, tok), BF16),
        vmem((TICKS, n, rows, tok), F32), vmem((TICKS, n, rows, tok), BF16),
        vmem((TICKS, n, rows, tok), F32),
        vmem((TICKS, n, rows, tok), BF16), vmem((TICKS, n, cols, tok), BF16),
        vmem((n, 1, tok), F32), vmem((TICKS, n, 1, tok), F32),
        vmem((rounds, n, n, 1, tok), F32),
        vmem((n, src, cols), F32), vmem((n, src, cols), F32),
        vmem((n, 1, cols), F32), vmem((ndp, n, 1, cols), F32),
        sem((n,)), sem((n,)), sem((n,)), sem((n,)), sem((n,)), sem((n,)), sem((n,)), sem((n,)),
        sem((rounds, 2, n)), sem((rounds, 2, n)), sem((ndp, n)), sem((ndp, n)), sem((3,)),
    ]
    in_vmem = pl.BlockSpec(memory_space=pltpu.VMEM)
    in_place = pl.BlockSpec(memory_space=pl.ANY)
    unroll = 8
    keys, values, gains = pl.pallas_call(
        functools.partial(kernel, n, ndp, unroll),
        out_shape=(
            jax.ShapeDtypeStruct((n, src, cols), BF16),
            jax.ShapeDtypeStruct((n, src, cols), BF16),
            jax.ShapeDtypeStruct((1, width), F32),
        ),
        in_specs=[in_vmem, in_place, in_vmem, in_vmem, in_vmem],
        out_specs=(in_vmem, in_vmem, in_vmem),
        scratch_shapes=scratch,
        compiler_params=pltpu.CompilerParams(
            collective_id=0, has_side_effects=True, vmem_limit_bytes=60 * 1024 * 1024),
    )(inputs[0, 0], cotangent[0, 0], key_rows[0], value_rows[0], query_gain)
    return keys[None], values[None], gains


def solution(mesh):
    return jax.shard_map(
        on_device,
        mesh=mesh,
        in_specs=(
            P("dp", "section", None, None),
            P("dp", None, None, "section"),
            P("dp", None, None, "section"),
            P("section", None),
            P("dp", "section", None, None),
        ),
        out_specs=(
            P("dp", None, None, "section"),
            P("dp", None, None, "section"),
            P("section", None),
        ),
        check_vma=False,
    )
```

profile of v0, /device:TPU:0, one launch (start us, length us, event | category | flops | bytes accessed | tf_op | source)
XLA Modules:
  0.0 60.8 jit_solution(17536774270067663544)
XLA Ops:
  0.6 57.2 %shard_map.76 = (bf16[8,24,512]{2,1,0:T(8,128)(2,1)}, bf16[8,24,512]{2,1,0:T(8,128)(2,1)}, f32[1,4096]{1,0:T(1,128)}) custom-call(bf16[128,4096]{1,0:T(8,128)(2,1)} %bitcast.6, bf16[128,4096]{1,0:T(8,128)(2,1)} %bitcast.7, bf16[8,24,512]{2,1,0:T(8,128)(2,1)} %bitcast.8, bf16[8,24,512]{2,1,0:T(8,128)(2,1)} %bitcast.9, f32[1,4096]{1,0:T(1,128)} %g_ref.1), custom_call_target="tpu_custom_call" | custom-call | tf_op jit(solution)/shard_map/pallas_call | solution.py:370
  57.8 0.0 copy-start
  57.8 1.7 %copy.11 = bf16[1,8,24,512]{3,2,1,0:T(8,128)(2,1)} copy(bf16[1,8,24,512]{3,2,1,0:T(8,128)(2,1)} %bitcast.11) | data formatting | bytes 393216
  59.5 0.0 copy-done
  59.5 0.0 copy-start.1
  59.5 0.7 %copy.12 = bf16[1,8,24,512]{3,2,1,0:T(8,128)(2,1)} copy(bf16[1,8,24,512]{3,2,1,0:T(8,128)(2,1)S(1)} %bitcast.10) | data formatting | bytes 393216
  60.2 0.0 copy-done.1
  60.2 0.6 copy.13
Async XLA Ops:
  57.8 1.7 %copy-start = (bf16[8,24,512]{2,1,0:T(8,128)(2,1)S(1)}, bf16[8,24,512]{2,1,0:T(8,128)(2,1)}, u32[]{:S(2)}) copy-start(bf16[8,24,512]{2,1,0:T(8,128)(2,1)} %get-tuple-element.7) | copy-start | bytes 589828
  59.5 0.7 %copy-start.1 = (f32[1,4096]{1,0:T(1,128)S(1)}, f32[1,4096]{1,0:T(1,128)}, u32[]{:S(2)}) copy-start(f32[1,4096]{1,0:T(1,128)} %get-tuple-element.14) | copy-start | bytes 49156
where the time goes:
time: 61.1 us; the launch traced here: 60.8 us
  Pallas kernels  57.2 us (94%)
  local copies, waits for them, and re-layouts  2.98 us (5%)
  between operations  0.65 us (1%)
    pallas_call x1, Pallas kernels, on_device(): pl.pallas_call(functools.partial(kernel, n, ndp, unroll), out_shape=(jax....  57.2 us
    unnamed x7, local copies, waits for them, and re-layouts  2.98 us

commit v1 on v0

--- a/solution.py
+++ b/solution.py
@@ -25,8 +25,9 @@
 
 def kernel(
     n, ndp, unroll,
-    x_ref, ct_ref, k_ref, v_ref, g_ref,
+    x_ref, ct_ref, k_in, v_in, g_ref,
     kout_ref, vout_ref, gout_ref,
+    x_own, k_ref, v_ref,
     xin, cin, gin, stat, kd, vd, kdt, vdt, gt, xs, qs, probs, plow, raws, ds, grads,
     red, inv, ar, ktot, vtot, gsend, gdp,
     x_send, x_recv, c_send, c_recv, g_send, g_recv, st_send, st_recv,
@@ -35,7 +36,7 @@
     me = lax.axis_index("section")
     doc = lax.axis_index("dp")
     tok, width = x_ref.shape
-    src, cols = k_ref.shape[1], k_ref.shape[2]
+    src, cols = k_in.shape[1], k_in.shape[2]
     blocks = cols // LANES
     per = LANES // HEAD
     brow = per * src
@@ -100,26 +101,33 @@
     others(lambda q, p: pl.semaphore_signal(
         barrier, inc=1, device_id={"dp": q, "section": p}, device_id_type=MESH))
 
-    total = jnp.zeros((tok, LANES), F32)
-    for b in range(width // LANES):
-        part = x_ref[:, b * LANES:(b + 1) * LANES].astype(F32)
-        total = total + part * part
-    stat[me] = jnp.sum(total.T, axis=0, keepdims=True)
-
-    pl.semaphore_wait(barrier, n * ndp - 1)
-
-    peers(lambda p: g_copy(p, me).start())
-    peers(lambda p: st_copy(p, me).start())
-    peers(lambda p: x_copy(p, me).start())
-    first_cut, second_cut = (1 + n) // 4, 1 + (5 * n) // 8
-    peers(lambda p: c_copy(p, me).start(), 1, first_cut)
     own = [
         pltpu.make_async_copy(cut(g_ref, me), gin.at[me], loc.at[0]),
         pltpu.make_async_copy(cut(x_ref, me), xin.at[me], loc.at[1]),
         pltpu.make_async_copy(cut(ct_ref, me), cin.at[me], loc.at[2]),
+        pltpu.make_async_copy(x_ref, x_own, loc.at[3]),
+        pltpu.make_async_copy(k_in, k_ref, loc.at[4]),
+        pltpu.make_async_copy(v_in, v_ref, loc.at[5]),
     ]
-    for copy in own:
-        copy.start()
+    for i in (3, 4, 5, 0, 1, 2):
+        own[i].start()
+
+    pl.semaphore_wait(barrier, n * ndp - 1)
+
+    peers(lambda p: x_copy(p, me).start(), 1, 2)
+    peers(lambda p: g_copy(p, me).start())
+    own[3].wait()
+    total = jnp.zeros((tok, LANES), F32)
+    for b in range(width // LANES):
+        part = x_own[:, b * LANES:(b + 1) * LANES].astype(F32)
+        total = total + part * part
+    stat[me] = jnp.sum(total.T, axis=0, keepdims=True)
+    peers(lambda p: st_copy(p, me).start())
+    peers(lambda p: x_copy(p, me).start(), 2)
+    first_cut, second_cut = (1 + n) // 4, 1 + (5 * n) // 8
+    peers(lambda p: c_copy(p, me).start(), 1, first_cut)
+    own[4].wait()
+    own[5].wait()
 
     lane = lax.broadcasted_iota(jnp.int32, (src, LANES), 1)
     sides = [jnp.logical_and(lane >= i * HEAD, lane < (i + 1) * HEAD) for i in range(per)]
@@ -336,6 +344,18 @@
         gout_ref[:, s * cols:(s + 1) * cols] = out
 
 
+def store(keys, values, gains, kout, vout, gout, done):
+    copies = [
+        pltpu.make_async_copy(keys, kout.at[0], done.at[0]),
+        pltpu.make_async_copy(values, vout.at[0], done.at[1]),
+        pltpu.make_async_copy(gains, gout, done.at[2]),
+    ]
+    for copy in copies:
+        copy.start()
+    for copy in copies:
+        copy.wait()
+
+
 def on_device(inputs, key_rows, value_rows, query_gain, cotangent):
     n = lax.axis_size("section")
     ndp = lax.axis_size("dp")
@@ -348,6 +368,7 @@
     vmem = pltpu.VMEM
     sem = pltpu.SemaphoreType.DMA
     scratch = [
+        vmem((tok, width), BF16), vmem((n, src, cols), BF16), vmem((n, src, cols), BF16),
         vmem((n, tok, cols), BF16), vmem((n, tok, cols), BF16),
         vmem((n, 1, cols), F32), vmem((n, 1, tok), F32),
         vmem((n, blocks, brow, LANES), BF16), vmem((n, blocks, brow, LANES), BF16),
@@ -362,7 +383,7 @@
         vmem((n, src, cols), F32), vmem((n, src, cols), F32),
         vmem((n, 1, cols), F32), vmem((ndp, n, 1, cols), F32),
         sem((n,)), sem((n,)), sem((n,)), sem((n,)), sem((n,)), sem((n,)), sem((n,)), sem((n,)),
-        sem((rounds, 2, n)), sem((rounds, 2, n)), sem((ndp, n)), sem((ndp, n)), sem((3,)),
+        sem((rounds, 2, n)), sem((rounds, 2, n)), sem((ndp, n)), sem((ndp, n)), sem((6,)),
     ]
     in_vmem = pl.BlockSpec(memory_space=pltpu.VMEM)
     in_place = pl.BlockSpec(memory_space=pl.ANY)
@@ -370,17 +391,28 @@
     keys, values, gains = pl.pallas_call(
         functools.partial(kernel, n, ndp, unroll),
         out_shape=(
-            jax.ShapeDtypeStruct((n, src, cols), BF16),
-            jax.ShapeDtypeStruct((n, src, cols), BF16),
-            jax.ShapeDtypeStruct((1, width), F32),
+            vmem((n, src, cols), BF16),
+            vmem((n, src, cols), BF16),
+            vmem((1, width), F32),
         ),
-        in_specs=[in_vmem, in_place, in_vmem, in_vmem, in_vmem],
+        in_specs=[in_place] * 5,
         out_specs=(in_vmem, in_vmem, in_vmem),
         scratch_shapes=scratch,
         compiler_params=pltpu.CompilerParams(
             collective_id=0, has_side_effects=True, vmem_limit_bytes=60 * 1024 * 1024),
     )(inputs[0, 0], cotangent[0, 0], key_rows[0], value_rows[0], query_gain)
-    return keys[None], values[None], gains
+    return pl.pallas_call(
+        store,
+        out_shape=(
+            jax.ShapeDtypeStruct((1, n, src, cols), BF16),
+            jax.ShapeDtypeStruct((1, n, src, cols), BF16),
+            jax.ShapeDtypeStruct((1, width), F32),
+        ),
+        in_specs=[in_place] * 3,
+        out_specs=(in_place,) * 3,
+        scratch_shapes=[sem((3,))],
+        compiler_params=pltpu.CompilerParams(vmem_limit_bytes=1024 * 1024),
+    )(keys, values, gains)
 
 
 def solution(mesh):

time: 61.1 us -> 57.2 us (0.936)
  local copies, waits for them, and re-layouts: 2.98 us -> 0 us
  Pallas kernels: 57.2 us -> 56.4 us
    unnamed x7 -> x0, local copies, waits for them, and re-layouts: 2.98 us -> none
    pallas_call x1 -> x2, Pallas kernels: 57.2 us -> 56.4 us  [the longest x1 55.6 us: on_device(): pl.pallas_call(functools.partial(kernel, n, ndp, unroll), out_shape=(vmem...]
where the time goes in v1:
time: 57.2 us; the launch traced here: 57 us
  Pallas kernels  56.4 us (99%)
  between operations  0.64 us (1%)
    pallas_call x1, Pallas kernels, on_device(): pl.pallas_call(functools.partial(kernel, n, ndp, unroll), out_shape=(vmem...  55.6 us

profile of v1, /device:TPU:0, one launch (start us, length us, event | category | flops | bytes accessed | tf_op | source)
XLA Modules:
  0.0 57.0 jit_solution(10895169449815237833)
XLA Ops:
  0.6 55.6 %shard_map.76 = (bf16[8,24,512]{2,1,0:T(8,128)(2,1)S(1)}, bf16[8,24,512]{2,1,0:T(8,128)(2,1)S(1)}, f32[1,4096]{1,0:T(1,128)S(1)}) custom-call(bf16[128,4096]{1,0:T(8,128)(2,1)} %bitcast.4, bf16[128,4096]{1,0:T(8,128)(2,1)} %bitcast.5, bf16[8,24,512]{2,1,0:T(8,128)(2,1)} %bitcast.6, bf16[8,24,512]{2,1,0:T(8,128)(2,1)} %bitcast.7, f32[1,4096]{1,0:T(1,128)} %g_ref.1), custom_call_target="tpu_custom_call" | custom-call | tf_op jit(solution)/shard_map/pallas_call | solution.py:391
  56.2 0.8 %shard_map.77 = (bf16[1,8,24,512]{3,2,1,0:T(8,128)(2,1)}, bf16[1,8,24,512]{3,2,1,0:T(8,128)(2,1)}, f32[1,4096]{1,0:T(1,128)}) custom-call(bf16[8,24,512]{2,1,0:T(8,128)(2,1)S(1)} %get-tuple-element.6.keys, bf16[8,24,512]{2,1,0:T(8,128)(2,1)S(1)} %get-tuple-element.7.values, f32[1,4096]{1,0:T(1,128)S(1)} %get-tuple-element.8.gains), custom_call_target="tpu_custom_call" | custom-call | tf_op jit(solution)/shard_map/pallas_call | solution.py:404

commit v2 on v1

--- a/solution.py
+++ b/solution.py
@@ -29,9 +29,9 @@
     kout_ref, vout_ref, gout_ref,
     x_own, k_ref, v_ref,
     xin, cin, gin, stat, kd, vd, kdt, vdt, gt, xs, qs, probs, plow, raws, ds, grads,
-    red, inv, ar, ktot, vtot, gsend, gdp,
+    wide, e1, e2, inv, ar, br, ktot, vtot, gsend, gdp,
     x_send, x_recv, c_send, c_recv, g_send, g_recv, st_send, st_recv,
-    ar_send, ar_recv, dp_send, dp_recv, loc,
+    ar_send, ar_recv, br_send, br_recv, dp_send, dp_recv, loc,
 ):
     me = lax.axis_index("section")
     doc = lax.axis_index("dp")
@@ -42,11 +42,19 @@
     brow = per * src
     scale = HEAD ** (-0.5)
 
+    def partner(j):
+        p = me
+        for b in range(n.bit_length() - 1):
+            if (j >> b) & 1:
+                p = p + (1 << b) - (2 << b) * lax.rem(lax.div(me, 1 << b), 2)
+        return p
+
+    order = sorted(range(n), key=lambda j: ((j >> 1).bit_count(), j & 1, j))
+    partners = [partner(j) for j in order]
+
     def peers(body, first=1, last=n):
-        def step(j, c):
-            body(lax.rem(me + j, n))
-            return c
-        lax.fori_loop(first, last, step, 0)
+        for p in partners[first:last]:
+            body(p)
 
     def each(body, first=0, last=n, u=None):
         def step(m, c):
@@ -87,6 +95,9 @@
     def ar_copy(a, h, p, slot):
         lo, hi = halves[h]
         return to(p, ar.at[a, me, lo:hi], ar.at[a, slot, lo:hi], ar_send.at[a, h, p], ar_recv.at[a, h, slot])
+
+    def br_copy(p, slot):
+        return to(p, br.at[:, me], br.at[:, slot], br_send.at[p], br_recv.at[slot])
 
     def share(a, h):
         peers(lambda p: ar_copy(a, h, p, me).start())
@@ -124,7 +135,7 @@
     stat[me] = jnp.sum(total.T, axis=0, keepdims=True)
     peers(lambda p: st_copy(p, me).start())
     peers(lambda p: x_copy(p, me).start(), 2)
-    first_cut, second_cut = (1 + n) // 4, 1 + (5 * n) // 8
+    first_cut, second_cut = n // 2, 3 * n // 4
     peers(lambda p: c_copy(p, me).start(), 1, first_cut)
     own[4].wait()
     own[5].wait()
@@ -155,6 +166,11 @@
 
     each(turn_gain, u=2)
     peers(lambda p: st_copy(p, p).wait_recv())
+
+    def softmax_back(p, dprob):
+        dprob = dprob.reshape(per, src, tok)
+        mean = jnp.sum(p * dprob, axis=1, keepdims=True)
+        return (p * (dprob - mean) * scale).reshape(brow, tok)
 
     def fwd(k, m, more):
         l = lax.rem(m + k, n)
@@ -181,8 +197,15 @@
                 xs[k + 1, m, at, :] = y
                 yf = y.astype(F32)
                 sums = sums + jnp.sum(yf * yf, axis=0, keepdims=True)
+            else:
+                before = probs[k - 1, m, rows, :].reshape(per, src, tok)
+                e = softmax_back(before, nn(vd[lax.rem(m + k - 1, n), b], xs[k, m, at, :]))
+                e2[m, rows, :] = e
+                sums = sums + jnp.sum(e * raws[k - 1, m, rows, :], axis=0, keepdims=True)
         if more:
             ar[k, me, m] = sums
+        else:
+            br[2, me, m] = sums
 
     def reduced(a, h):
         lo, hi = halves[h]
@@ -192,15 +215,11 @@
             total = total + ar[a, s, lo:hi]
         return total * (1.0 / width)
 
-    def arrive(j, c):
-        m = lax.rem(me + j, n)
-
-        @pl.when(j == 0)
-        def _():
+    def arrive(j):
+        m = partners[j]
+        if j == 0:
             own[1].wait()
-
-        @pl.when(j > 0)
-        def _():
+        else:
             x_copy(m, m).wait_recv()
 
         inv[0, m] = lax.rsqrt(stat[m] * (1.0 / width) + 1e-6)
@@ -208,9 +227,9 @@
             at = slice(b * LANES, (b + 1) * LANES)
             xs[0, m, at, :] = xin[m, :, at].T
         fwd(0, m, True)
-        return c
-
-    lax.fori_loop(0, n, arrive, 0)
+
+    for j in range(n):
+        arrive(j)
     share(0, 0)
     share(0, 1)
     peers(lambda p: c_copy(p, me).start(), first_cut, second_cut)
@@ -223,8 +242,6 @@
         if k == 1:
             peers(lambda p: c_copy(p, me).start(), second_cut, n)
 
-    own[2].wait()
-
     def arrive_c(p):
         c_copy(p, p).wait_recv()
 
@@ -234,23 +251,29 @@
             at = slice(b * LANES, (b + 1) * LANES)
             grads[TICKS - 1, m, at, :] = cin[s, :, at].T
 
-    peers(arrive_c)
-
-    def scores_back(k, a, m):
+    def start_back(m):
+        k = TICKS - 1
         l = lax.rem(m + k, n)
+        earlier = lax.rem(m + k - 1, n)
+        factor = inv[k, m]
         sums = jnp.zeros((1, tok), F32)
+        ahead = jnp.zeros((1, tok), F32)
         for b in range(blocks):
             at = slice(b * LANES, (b + 1) * LANES)
             rows = slice(b * brow, (b + 1) * brow)
-            dprob = nn(vd[l, b], grads[k, m, at, :]).reshape(per, src, tok)
+            g = grads[k, m, at, :]
             p = probs[k, m, rows, :].reshape(per, src, tok)
-            mean = jnp.sum(p * dprob, axis=1, keepdims=True)
-            d = (p * (dprob - mean) * scale).reshape(brow, tok).astype(BF16)
+            d = softmax_back(p, nn(vd[l, b], g)).astype(BF16)
             ds[k, m, rows, :] = d
-            if a is not None:
-                sums = sums + jnp.sum(d.astype(F32) * raws[k, m, rows, :], axis=0, keepdims=True)
-        if a is not None:
-            ar[a, me, m] = sums
+            sums = sums + jnp.sum(d.astype(F32) * raws[k, m, rows, :], axis=0, keepdims=True)
+            h = g.astype(F32) + factor * (gt[l, at, :] * nn(kdt[l, b], d))
+            wide[m, at, :] = h
+            p = probs[k - 1, m, rows, :].reshape(per, src, tok)
+            e = softmax_back(p, nn(vd[earlier, b], h.astype(BF16)))
+            e1[m, rows, :] = e
+            ahead = ahead + jnp.sum(e * raws[k - 1, m, rows, :], axis=0, keepdims=True)
+        br[0, me, m] = sums
+        br[1, me, m] = ahead
 
     def picked(r):
         out = r[:src]
@@ -272,38 +295,46 @@
             rows = slice(b * brow, (b + 1) * brow)
             vtot[l, :, at] += picked(nt(plow[k, m, rows, :], grads[k, m, at, :]))
 
-    def input_back(k, m):
-        l = lax.rem(m + k, n)
-        factor = inv[k, m]
-        mean = red[m]
+    def mean_of(a, m):
+        total = br[a, 0, m]
+        for j in range(1, n):
+            total = total + br[a, j, m]
+        return total * (1.0 / width)
+
+    def finish_back(m):
+        l1 = lax.rem(m + 1, n)
+        late, early = inv[2, m], inv[1, m]
+        c = late * late * mean_of(0, m)
+        mean = mean_of(1, m) - c * mean_of(2, m)
         for b in range(blocks):
             at = slice(b * LANES, (b + 1) * LANES)
             rows = slice(b * brow, (b + 1) * brow)
-            dq = nn(kdt[l, b], ds[k, m, rows, :])
-            u = xs[k, m, at, :].astype(F32) * factor
-            back = grads[k, m, at, :].astype(F32) + factor * (gt[l, at, :] * dq - u * mean)
-            grads[k - 1, m, at, :] = back.astype(BF16)
-
-    def start_back(m):
+            g = (wide[m, at, :] - c * xs[2, m, at, :].astype(F32)).astype(BF16)
+            grads[1, m, at, :] = g
+            d = (e1[m, rows, :] - c * e2[m, rows, :]).astype(BF16)
+            ds[1, m, rows, :] = d
+            u = xs[1, m, at, :].astype(F32) * early
+            g = g.astype(F32) + early * (gt[l1, at, :] * nn(kdt[l1, b], d) - u * mean)
+            g = g.astype(BF16)
+            grads[0, m, at, :] = g
+            p = probs[0, m, rows, :].reshape(per, src, tok)
+            ds[0, m, rows, :] = softmax_back(p, nn(vd[m, b], g)).astype(BF16)
+
+    for j in range(n):
+        p = partners[j]
+        if j == 0:
+            own[2].wait()
+        else:
+            arrive_c(p)
+        m = lax.rem(p + n - TICKS % n, n)
         turn_c(m)
-        scores_back(TICKS - 1, 2 * TICKS - 3, m)
-
-    for h, (lo, hi) in enumerate(halves):
-        each(start_back, lo, hi)
-        share(2 * TICKS - 3, h)
-    for k in range(TICKS - 1, 0, -1):
-        a = TICKS - 1 + k - 1
-
-        def next_back(m):
-            input_back(k, m)
-            scores_back(k - 1, a - 1 if k > 1 else None, m)
-
-        each(lambda m: key_step(k, m))
-        for h, (lo, hi) in enumerate(halves):
-            red[lo:hi] = reduced(a, h)
-            each(next_back, lo, hi)
-            if k > 1:
-                share(a - 1, h)
+        start_back(m)
+    peers(lambda p: br_copy(p, me).start())
+    each(lambda m: key_step(2, m))
+    each(lambda m: value_step(2, m))
+    peers(lambda p: br_copy(p, p).wait_recv())
+    each(finish_back)
+    each(lambda m: key_step(1, m))
 
     def last(m):
         key_step(0, m)
@@ -315,9 +346,7 @@
     others(lambda q, p: dp_copy(q, p, doc, me).start())
     gdp[doc, me] = gsend[me]
 
-    each(lambda m: value_step(TICKS - 1, m))
-    for k in range(1, TICKS - 1):
-        each(lambda m: value_step(k, m))
+    each(lambda m: value_step(1, m))
 
     def finish(m):
         value_step(0, m)
@@ -330,7 +359,8 @@
         c_copy(p, me).wait_send()
         g_copy(p, me).wait_send()
         st_copy(p, me).wait_send()
-        for a in range(2 * (TICKS - 1)):
+        br_copy(p, me).wait_send()
+        for a in range(TICKS - 1):
             for h in range(2):
                 ar_copy(a, h, p, me).wait_send()
 
@@ -364,7 +394,7 @@
     blocks = cols // LANES
     brow = LANES // HEAD * src
     rows = blocks * brow
-    rounds = 2 * (TICKS - 1)
+    rounds = TICKS - 1
     vmem = pltpu.VMEM
     sem = pltpu.SemaphoreType.DMA
     scratch = [
@@ -378,12 +408,13 @@
         vmem((TICKS, n, rows, tok), F32), vmem((TICKS, n, rows, tok), BF16),
         vmem((TICKS, n, rows, tok), F32),
         vmem((TICKS, n, rows, tok), BF16), vmem((TICKS, n, cols, tok), BF16),
-        vmem((n, 1, tok), F32), vmem((TICKS, n, 1, tok), F32),
-        vmem((rounds, n, n, 1, tok), F32),
+        vmem((n, cols, tok), F32), vmem((n, rows, tok), F32), vmem((n, rows, tok), F32),
+        vmem((TICKS, n, 1, tok), F32),
+        vmem((rounds, n, n, 1, tok), F32), vmem((3, n, n, 1, tok), F32),
         vmem((n, src, cols), F32), vmem((n, src, cols), F32),
         vmem((n, 1, cols), F32), vmem((ndp, n, 1, cols), F32),
         sem((n,)), sem((n,)), sem((n,)), sem((n,)), sem((n,)), sem((n,)), sem((n,)), sem((n,)),
-        sem((rounds, 2, n)), sem((rounds, 2, n)), sem((ndp, n)), sem((ndp, n)), sem((6,)),
+        sem((rounds, 2, n)), sem((rounds, 2, n)), sem((n,)), sem((n,)), sem((ndp, n)), sem((ndp, n)), sem((6,)),
     ]
     in_vmem = pl.BlockSpec(memory_space=pltpu.VMEM)
     in_place = pl.BlockSpec(memory_space=pl.ANY)

time: 57.2 us -> 51.4 us (0.90)
  Pallas kernels: 56.4 us -> 50.7 us
    pallas_call x1, Pallas kernels: 55.6 us -> 49.9 us  [on_device(): pl.pallas_call(functools.partial(kernel, n, ndp, unroll), out_shape=(vmem...]
where the time goes in v2:
time: 51.4 us; the launch traced here: 51.3 us
  Pallas kernels  50.7 us (99%)
  between operations  0.64 us (1%)
    pallas_call x1, Pallas kernels, on_device(): pl.pallas_call(functools.partial(kernel, n, ndp, unroll), out_shape=(vmem...  49.9 us

profile of v2, /device:TPU:0, one launch (start us, length us, event | category | flops | bytes accessed | tf_op | source)
XLA Modules:
  0.0 51.3 jit_solution(11802155847764126446)
XLA Ops:
  0.6 49.9 %shard_map.76 = (bf16[8,24,512]{2,1,0:T(8,128)(2,1)S(1)}, bf16[8,24,512]{2,1,0:T(8,128)(2,1)S(1)}, f32[1,4096]{1,0:T(1,128)S(1)}) custom-call(bf16[128,4096]{1,0:T(8,128)(2,1)} %bitcast.4, bf16[128,4096]{1,0:T(8,128)(2,1)} %bitcast.5, bf16[8,24,512]{2,1,0:T(8,128)(2,1)} %bitcast.6, bf16[8,24,512]{2,1,0:T(8,128)(2,1)} %bitcast.7, f32[1,4096]{1,0:T(1,128)} %g_ref.1), custom_call_target="tpu_custom_call" | custom-call | tf_op jit(solution)/shard_map/pallas_call | solution.py:422
  50.5 0.8 %shard_map.77 = (bf16[1,8,24,512]{3,2,1,0:T(8,128)(2,1)}, bf16[1,8,24,512]{3,2,1,0:T(8,128)(2,1)}, f32[1,4096]{1,0:T(1,128)}) custom-call(bf16[8,24,512]{2,1,0:T(8,128)(2,1)S(1)} %get-tuple-element.6.keys, bf16[8,24,512]{2,1,0:T(8,128)(2,1)S(1)} %get-tuple-element.7.values, f32[1,4096]{1,0:T(1,128)S(1)} %get-tuple-element.8.gains), custom_call_target="tpu_custom_call" | custom-call | tf_op jit(solution)/shard_map/pallas_call | solution.py:435

commit v3 on v2

--- a/solution.py
+++ b/solution.py
@@ -83,8 +83,20 @@
     def x_copy(p, slot):
         return to(p, cut(x_ref, p), xin.at[slot], x_send.at[p], x_recv.at[slot])
 
-    def c_copy(p, slot):
-        return to(p, cut(ct_ref, p), cin.at[slot], c_send.at[p], c_recv.at[slot])
+    def c_copy(p, slot, part):
+        rows = pl.ds(part * (tok // 2), tok // 2)
+        source = ct_ref.at[rows, pl.ds(pl.multiple_of(p * cols, LANES), cols)]
+        return to(p, source, cin.at[slot, rows], c_send.at[part, p], c_recv.at[part, slot])
+
+    units = []
+    for j in range(1, n - 1, 2):
+        units += [(j, 0), (j + 1, 0), (j, 1), (j + 1, 1)]
+    units = [(1, 0), (1, 1)] + [(j + 1, part) for j, part in units]
+    units = [(j, part) for j, part in units if j < n]
+
+    def c_send_units(lo, hi):
+        for j, part in units[lo:hi]:
+            c_copy(partners[j], me, part).start()
 
     def g_copy(p, slot):
         return to(p, cut(g_ref, p), gin.at[slot], g_send.at[p], g_recv.at[slot])
@@ -105,7 +117,7 @@
     def dp_copy(q, p, from_doc, slot):
         return pltpu.make_async_remote_copy(
             src_ref=gsend.at[p], dst_ref=gdp.at[from_doc, slot],
-            send_sem=dp_send.at[q, p], recv_sem=dp_recv.at[from_doc, slot],
+            send_sem=dp_send, recv_sem=dp_recv,
             device_id={"dp": q, "section": p}, device_id_type=MESH)
 
     barrier = pltpu.get_barrier_semaphore()
@@ -125,8 +137,8 @@
 
     pl.semaphore_wait(barrier, n * ndp - 1)
 
-    peers(lambda p: x_copy(p, me).start(), 1, 2)
     peers(lambda p: g_copy(p, me).start())
+    peers(lambda p: x_copy(p, me).start(), 1, n // 2)
     own[3].wait()
     total = jnp.zeros((tok, LANES), F32)
     for b in range(width // LANES):
@@ -134,9 +146,9 @@
         total = total + part * part
     stat[me] = jnp.sum(total.T, axis=0, keepdims=True)
     peers(lambda p: st_copy(p, me).start())
-    peers(lambda p: x_copy(p, me).start(), 2)
-    first_cut, second_cut = n // 2, 3 * n // 4
-    peers(lambda p: c_copy(p, me).start(), 1, first_cut)
+    peers(lambda p: x_copy(p, me).start(), n // 2)
+    first_cut, second_cut = n - 2, n + 2
+    c_send_units(0, first_cut)
     own[4].wait()
     own[5].wait()
 
@@ -232,7 +244,7 @@
         arrive(j)
     share(0, 0)
     share(0, 1)
-    peers(lambda p: c_copy(p, me).start(), first_cut, second_cut)
+    c_send_units(first_cut, second_cut)
     for k in range(1, TICKS):
         for h, (lo, hi) in enumerate(halves):
             inv[k, lo:hi] = lax.rsqrt(reduced(k - 1, h) + 1e-6)
@@ -240,10 +252,11 @@
             if k + 1 < TICKS:
                 share(k, h)
         if k == 1:
-            peers(lambda p: c_copy(p, me).start(), second_cut, n)
+            c_send_units(second_cut, len(units))
 
     def arrive_c(p):
-        c_copy(p, p).wait_recv()
+        c_copy(p, p, 0).wait_recv()
+        c_copy(p, p, 1).wait_recv()
 
     def turn_c(m):
         s = lax.rem(m + TICKS, n)
@@ -287,6 +300,18 @@
             at = slice(b * LANES, (b + 1) * LANES)
             rows = slice(b * brow, (b + 1) * brow)
             ktot[l, :, at] += picked(nt(ds[k, m, rows, :], qs[k, m, at, :]))
+
+    def pair(ref, l, rows):
+        return jnp.concatenate(
+            [ref[1, lax.rem(l + n - 1, n), rows, :], ref[0, l, rows, :]], axis=1)
+
+    def paired(left, right, l):
+        out = []
+        for b in range(blocks):
+            at = slice(b * LANES, (b + 1) * LANES)
+            rows = slice(b * brow, (b + 1) * brow)
+            out.append(picked(nt(pair(left, l, rows), pair(right, l, at))))
+        return jnp.concatenate(out, axis=1)
 
     def value_step(k, m):
         l = lax.rem(m + k, n)
@@ -334,29 +359,26 @@
     each(lambda m: value_step(2, m))
     peers(lambda p: br_copy(p, p).wait_recv())
     each(finish_back)
-    each(lambda m: key_step(1, m))
-
-    def last(m):
-        key_step(0, m)
-        steps = ktot[m]
-        kout_ref[m] = steps.astype(BF16)
-        gsend[m] = jnp.sum(steps * k_ref[m].astype(F32), axis=0, keepdims=True) / gin[m]
+
+    def last(l):
+        steps = ktot[l] + paired(ds, qs, l)
+        kout_ref[l] = steps.astype(BF16)
+        gsend[l] = jnp.sum(steps * k_ref[l].astype(F32), axis=0, keepdims=True) / gin[l]
 
     each(last)
+    own_gain = pltpu.make_async_copy(gsend.at[me], gdp.at[doc, me], dp_recv)
     others(lambda q, p: dp_copy(q, p, doc, me).start())
-    gdp[doc, me] = gsend[me]
-
-    each(lambda m: value_step(1, m))
-
-    def finish(m):
-        value_step(0, m)
-        vout_ref[m] = vtot[m].astype(BF16)
+    own_gain.start()
+
+    def finish(l):
+        vout_ref[l] = (vtot[l] + paired(plow, grads, l)).astype(BF16)
 
     each(finish)
 
     def drain(p):
         x_copy(p, me).wait_send()
-        c_copy(p, me).wait_send()
+        c_copy(p, me, 0).wait_send()
+        c_copy(p, me, 1).wait_send()
         g_copy(p, me).wait_send()
         st_copy(p, me).wait_send()
         br_copy(p, me).wait_send()
@@ -365,8 +387,10 @@
                 ar_copy(a, h, p, me).wait_send()
 
     peers(drain)
-    others(lambda q, p: dp_copy(q, p, q, p).wait_recv())
-    others(lambda q, p: dp_copy(q, p, doc, me).wait_send())
+    pltpu.make_async_copy(gdp, gdp, dp_recv).wait()
+    for d in range(ndp - 1):
+        pltpu.make_async_copy(gdp.at[d], gdp.at[d], dp_send).wait()
+    pltpu.make_async_copy(gdp.at[0, 1:], gdp.at[0, 1:], dp_send).wait()
     for s in range(n):
         out = gdp[0, s]
         for d in range(1, ndp):
@@ -413,8 +437,8 @@
         vmem((rounds, n, n, 1, tok), F32), vmem((3, n, n, 1, tok), F32),
         vmem((n, src, cols), F32), vmem((n, src, cols), F32),
         vmem((n, 1, cols), F32), vmem((ndp, n, 1, cols), F32),
-        sem((n,)), sem((n,)), sem((n,)), sem((n,)), sem((n,)), sem((n,)), sem((n,)), sem((n,)),
-        sem((rounds, 2, n)), sem((rounds, 2, n)), sem((n,)), sem((n,)), sem((ndp, n)), sem((ndp, n)), sem((6,)),
+        sem((n,)), sem((n,)), sem((2, n)), sem((2, n)), sem((n,)), sem((n,)), sem((n,)), sem((n,)),
+        sem((rounds, 2, n)), sem((rounds, 2, n)), sem((n,)), sem((n,)), sem(()), sem(()), sem((6,)),
     ]
     in_vmem = pl.BlockSpec(memory_space=pltpu.VMEM)
     in_place = pl.BlockSpec(memory_space=pl.ANY)

time: 51.4 us -> 49.8 us (0.969)
  Pallas kernels: 50.7 us -> 49 us
    pallas_call x1, Pallas kernels: 49.9 us -> 48.3 us  [on_device(): pl.pallas_call(functools.partial(kernel, n, ndp, unroll), out_shape=(vmem...]
where the time goes in v3:
time: 49.8 us; the launch traced here: 49.7 us
  Pallas kernels  49 us (98%)
  between operations  0.64 us (1%)
    pallas_call x1, Pallas kernels, on_device(): pl.pallas_call(functools.partial(kernel, n, ndp, unroll), out_shape=(vmem...  48.3 us

profile of v3, /device:TPU:0, one launch (start us, length us, event | category | flops | bytes accessed | tf_op | source)
XLA Modules:
  0.0 49.7 jit_solution(16676481979499350294)
XLA Ops:
  0.6 48.3 %shard_map.76 = (bf16[8,24,512]{2,1,0:T(8,128)(2,1)S(1)}, bf16[8,24,512]{2,1,0:T(8,128)(2,1)S(1)}, f32[1,4096]{1,0:T(1,128)S(1)}) custom-call(bf16[128,4096]{1,0:T(8,128)(2,1)} %bitcast.4, bf16[128,4096]{1,0:T(8,128)(2,1)} %bitcast.5, bf16[8,24,512]{2,1,0:T(8,128)(2,1)} %bitcast.6, bf16[8,24,512]{2,1,0:T(8,128)(2,1)} %bitcast.7, f32[1,4096]{1,0:T(1,128)} %g_ref.1), custom_call_target="tpu_custom_call" | custom-call | tf_op jit(solution)/shard_map/pallas_call | solution.py:446
  48.9 0.8 %shard_map.77 = (bf16[1,8,24,512]{3,2,1,0:T(8,128)(2,1)}, bf16[1,8,24,512]{3,2,1,0:T(8,128)(2,1)}, f32[1,4096]{1,0:T(1,128)}) custom-call(bf16[8,24,512]{2,1,0:T(8,128)(2,1)S(1)} %get-tuple-element.6.keys, bf16[8,24,512]{2,1,0:T(8,128)(2,1)S(1)} %get-tuple-element.7.values, f32[1,4096]{1,0:T(1,128)S(1)} %get-tuple-element.8.gains), custom_call_target="tpu_custom_call" | custom-call | tf_op jit(solution)/shard_map/pallas_call | solution.py:459

commit v4 on v3

--- a/solution.py
+++ b/solution.py
@@ -42,6 +42,19 @@
     brow = per * src
     scale = HEAD ** (-0.5)
 
+    share_of = 2 if blocks % 2 == 0 else 1
+    groups = [tuple(range(b, b + share_of)) for b in range(0, blocks, share_of)]
+
+    singles = [(b,) for b in range(blocks)]
+
+    def span(b):
+        return slice(b * LANES, (b + 1) * LANES), slice(b * brow, (b + 1) * brow)
+
+    def products(table, l, group, rights):
+        left = jnp.concatenate([table[l, b] for b in group], axis=0)
+        out = nn(left, jnp.concatenate(rights, axis=1))
+        return [out[i * brow:(i + 1) * brow, i * tok:(i + 1) * tok] for i in range(len(group))]
+
     def partner(j):
         p = me
         for b in range(n.bit_length() - 1):
@@ -52,6 +65,12 @@
     order = sorted(range(n), key=lambda j: ((j >> 1).bit_count(), j & 1, j))
     partners = [partner(j) for j in order]
 
+    def across(p):
+        v = 0
+        for b in range(n.bit_length() - 1):
+            v = v + (1 << b) * lax.rem(lax.div(me, 1 << b) + lax.div(p, 1 << b), 2)
+        return v
+
     def peers(body, first=1, last=n):
         for p in partners[first:last]:
             body(p)
@@ -88,11 +107,10 @@
         source = ct_ref.at[rows, pl.ds(pl.multiple_of(p * cols, LANES), cols)]
         return to(p, source, cin.at[slot, rows], c_send.at[part, p], c_recv.at[part, slot])
 
-    units = []
-    for j in range(1, n - 1, 2):
+    units = [(1, 0), (1, 1)]
+    for j in range(2, n - 2, 2):
         units += [(j, 0), (j + 1, 0), (j, 1), (j + 1, 1)]
-    units = [(1, 0), (1, 1)] + [(j + 1, part) for j, part in units]
-    units = [(j, part) for j, part in units if j < n]
+    units += [(j, part) for j in (n - 2, n - 1) for part in (0, 1)]
 
     def c_send_units(lo, hi):
         for j, part in units[lo:hi]:
@@ -163,8 +181,6 @@
                 both = jnp.concatenate([jnp.where(s, piece, 0.0) for s in sides], axis=0)
                 plain[l, b] = both.astype(BF16)
                 turned[l, b] = both.T.astype(BF16)
-        ktot[l] = jnp.zeros((src, cols), F32)
-        vtot[l] = jnp.zeros((src, cols), F32)
 
     each(spread, u=2)
 
@@ -184,40 +200,49 @@
         mean = jnp.sum(p * dprob, axis=1, keepdims=True)
         return (p * (dprob - mean) * scale).reshape(brow, tok)
 
-    def fwd(k, m, more):
+    def fwd(k, m, more, states=None):
         l = lax.rem(m + k, n)
         factor = inv[k, m]
         pieces = []
         sums = jnp.zeros((1, tok), F32)
-        for b in range(blocks):
-            at = slice(b * LANES, (b + 1) * LANES)
-            rows = slice(b * brow, (b + 1) * brow)
-            xf = xs[k, m, at, :].astype(F32)
-            q = (xf * factor * gt[l, at, :]).astype(BF16)
-            qs[k, m, at, :] = q
-            raw = nn(kd[l, b], q)
-            raws[k, m, rows, :] = raw
-            s3 = raw.reshape(per, src, tok) * scale
-            w = jnp.exp(s3 - jnp.max(s3, axis=1, keepdims=True))
-            p = w * (1.0 / jnp.sum(w, axis=1, keepdims=True))
-            p = p.reshape(brow, tok)
-            probs[k, m, rows, :] = p
-            low = p.astype(BF16)
-            plow[k, m, rows, :] = low
-            if more:
-                y = (xf + nn(vdt[l, b], low)).astype(BF16)
-                xs[k + 1, m, at, :] = y
-                yf = y.astype(F32)
-                sums = sums + jnp.sum(yf * yf, axis=0, keepdims=True)
-            else:
-                before = probs[k - 1, m, rows, :].reshape(per, src, tok)
-                e = softmax_back(before, nn(vd[lax.rem(m + k - 1, n), b], xs[k, m, at, :]))
-                e2[m, rows, :] = e
-                sums = sums + jnp.sum(e * raws[k - 1, m, rows, :], axis=0, keepdims=True)
+        for group in singles:
+            xfs, queries = [], []
+            for b in group:
+                at, _ = span(b)
+                xf = (xs[k, m, at, :] if states is None else states[b]).astype(F32)
+                q = (xf * factor * gt[l, at, :]).astype(BF16)
+                qs[k, m, at, :] = q
+                xfs.append(xf)
+                queries.append(q)
+            scores = products(kd, l, group, queries)
+            for b, xf, raw in zip(group, xfs, scores):
+                at, rows = span(b)
+                raws[k, m, rows, :] = raw
+                s3 = raw.reshape(per, src, tok) * scale
+                w = jnp.exp(s3 - jnp.max(s3, axis=1, keepdims=True))
+                p = w * (1.0 / jnp.sum(w, axis=1, keepdims=True))
+                p = p.reshape(brow, tok)
+                probs[k, m, rows, :] = p
+                low = p.astype(BF16)
+                plow[k, m, rows, :] = low
+                if more:
+                    y = (xf + nn(vdt[l, b], low)).astype(BF16)
+                    xs[k + 1, m, at, :] = y
+                    yf = y.astype(F32)
+                    sums = sums + jnp.sum(yf * yf, axis=0, keepdims=True)
         if more:
             ar[k, me, m] = sums
-        else:
-            br[2, me, m] = sums
+
+    def response(m):
+        sums = jnp.zeros((1, tok), F32)
+        for group in groups:
+            out = products(vd, lax.rem(m + 1, n), group, [xs[2, m, span(b)[0], :] for b in group])
+            for b, dprob in zip(group, out):
+                _, rows = span(b)
+                e = softmax_back(probs[1, m, rows, :].reshape(per, src, tok), dprob)
+                e2[m, rows, :] = e
+                sums = sums + jnp.sum(e * raws[1, m, rows, :], axis=0, keepdims=True)
+        br[2, me, m] = sums
 
     def reduced(a, h):
         lo, hi = halves[h]
@@ -235,16 +260,40 @@
             x_copy(m, m).wait_recv()
 
         inv[0, m] = lax.rsqrt(stat[m] * (1.0 / width) + 1e-6)
+        states = [xin[m, :, b * LANES:(b + 1) * LANES].T for b in range(blocks)]
         for b in range(blocks):
-            at = slice(b * LANES, (b + 1) * LANES)
-            xs[0, m, at, :] = xin[m, :, at].T
-        fwd(0, m, True)
+            xs[0, m, b * LANES:(b + 1) * LANES, :] = states[b]
+        fwd(0, m, True, states)
+
+    def arrive_c(j):
+        p = partners[j]
+        if j == 0:
+            own[2].wait()
+        else:
+            c_copy(p, p, 0).wait_recv()
+            c_copy(p, p, 1).wait_recv()
+
+    def chain_of(j):
+        return lax.rem(partners[j] + n - TICKS % n, n)
+
+    def turn_c(j):
+        turned = [cin[partners[j], :, b * LANES:(b + 1) * LANES].T for b in range(blocks)]
+        for b in range(blocks):
+            grads[TICKS - 1, order[j], b * LANES:(b + 1) * LANES, :] = turned[b]
+        return turned
+
+    def turn_early(lo, hi):
+        for j in range(lo, hi):
+            arrive_c(j)
+        for j in range(lo, hi):
+            turn_c(j)
 
     for j in range(n):
         arrive(j)
     share(0, 0)
     share(0, 1)
     c_send_units(first_cut, second_cut)
+    turn_early(0, n // 4)
     for k in range(1, TICKS):
         for h, (lo, hi) in enumerate(halves):
             inv[k, lo:hi] = lax.rsqrt(reduced(k - 1, h) + 1e-6)
@@ -253,40 +302,41 @@
                 share(k, h)
         if k == 1:
             c_send_units(second_cut, len(units))
-
-    def arrive_c(p):
-        c_copy(p, p, 0).wait_recv()
-        c_copy(p, p, 1).wait_recv()
-
-    def turn_c(m):
-        s = lax.rem(m + TICKS, n)
-        for b in range(blocks):
-            at = slice(b * LANES, (b + 1) * LANES)
-            grads[TICKS - 1, m, at, :] = cin[s, :, at].T
-
-    def start_back(m):
+            each(response)
+            turn_early(n // 4, n // 2)
+
+    def start_back(j, turned=None):
+        m, v = chain_of(j), order[j]
         k = TICKS - 1
         l = lax.rem(m + k, n)
         earlier = lax.rem(m + k - 1, n)
         factor = inv[k, m]
         sums = jnp.zeros((1, tok), F32)
         ahead = jnp.zeros((1, tok), F32)
-        for b in range(blocks):
-            at = slice(b * LANES, (b + 1) * LANES)
-            rows = slice(b * brow, (b + 1) * brow)
-            g = grads[k, m, at, :]
-            p = probs[k, m, rows, :].reshape(per, src, tok)
-            d = softmax_back(p, nn(vd[l, b], g)).astype(BF16)
-            ds[k, m, rows, :] = d
-            sums = sums + jnp.sum(d.astype(F32) * raws[k, m, rows, :], axis=0, keepdims=True)
-            h = g.astype(F32) + factor * (gt[l, at, :] * nn(kdt[l, b], d))
-            wide[m, at, :] = h
-            p = probs[k - 1, m, rows, :].reshape(per, src, tok)
-            e = softmax_back(p, nn(vd[earlier, b], h.astype(BF16)))
-            e1[m, rows, :] = e
-            ahead = ahead + jnp.sum(e * raws[k - 1, m, rows, :], axis=0, keepdims=True)
-        br[0, me, m] = sums
-        br[1, me, m] = ahead
+        for group in groups:
+            gs = [grads[k, v, span(b)[0], :] if turned is None else turned[b] for b in group]
+            hs = []
+            for b, g, dprob in zip(group, gs, products(vd, l, group, gs)):
+                at, rows = span(b)
+                p = probs[k, m, rows, :].reshape(per, src, tok)
+                d = softmax_back(p, dprob).astype(BF16)
+                ds[k, v, rows, :] = d
+                sums = sums + jnp.sum(d.astype(F32) * raws[k, m, rows, :], axis=0, keepdims=True)
+                h = g.astype(F32) + factor * (gt[l, at, :] * nn(kdt[l, b], d))
+                wide[v, at, :] = h
+                hs.append(h.astype(BF16))
+            for b, dprob in zip(group, products(vd, earlier, group, hs)):
+                _, rows = span(b)
+                p = probs[k - 1, m, rows, :].reshape(per, src, tok)
+                e = softmax_back(p, dprob)
+                e1[v, rows, :] = e
+                ahead = ahead + jnp.sum(e * raws[k - 1, m, rows, :], axis=0, keepdims=True)
+        return m, sums, ahead
+
+    def keep(rows_of):
+        for m, sums, ahead in rows_of:
+            br[0, me, m] = sums
+            br[1, me, m] = ahead
 
     def picked(r):
         out = r[:src]
@@ -294,31 +344,31 @@
             out = jnp.where(sides[i], r[i * src:(i + 1) * src], out)
         return out
 
-    def key_step(k, m):
-        l = lax.rem(m + k, n)
-        for b in range(blocks):
-            at = slice(b * LANES, (b + 1) * LANES)
-            rows = slice(b * brow, (b + 1) * brow)
-            ktot[l, :, at] += picked(nt(ds[k, m, rows, :], qs[k, m, at, :]))
-
-    def pair(ref, l, rows):
-        return jnp.concatenate(
-            [ref[1, lax.rem(l + n - 1, n), rows, :], ref[0, l, rows, :]], axis=1)
-
-    def paired(left, right, l):
+    spot = [across((m + TICKS) % n) for m in range(n)]
+
+    def steps(left, right, l):
         out = []
-        for b in range(blocks):
-            at = slice(b * LANES, (b + 1) * LANES)
-            rows = slice(b * brow, (b + 1) * brow)
-            out.append(picked(nt(pair(left, l, rows), pair(right, l, at))))
+        for group in groups:
+            rows = slice(group[0] * brow, (group[-1] + 1) * brow)
+            at = slice(group[0] * LANES, (group[-1] + 1) * LANES)
+            r = nt(left(l, rows), right(l, at))
+            for i in range(len(group)):
+                out.append(picked(r[i * brow:(i + 1) * brow, i * LANES:(i + 1) * LANES]))
         return jnp.concatenate(out, axis=1)
 
-    def value_step(k, m):
-        l = lax.rem(m + k, n)
-        for b in range(blocks):
-            at = slice(b * LANES, (b + 1) * LANES)
-            rows = slice(b * brow, (b + 1) * brow)
-            vtot[l, :, at] += picked(nt(plow[k, m, rows, :], grads[k, m, at, :]))
+    def of_chain(ref):
+        return lambda l, rows: ref[2, (l - 2) % n, rows, :]
+
+    def of_spot(ref):
+        return lambda l, rows: ref[2, spot[(l - 2) % n], rows, :]
+
+    def pair_of_chain(ref):
+        return lambda l, rows: jnp.concatenate(
+            [ref[1, (l - 1) % n, rows, :], ref[0, l, rows, :]], axis=1)
+
+    def pair_of_spot(ref):
+        return lambda l, rows: jnp.concatenate(
+            [ref[1, spot[(l - 1) % n], rows, :], ref[0, spot[l], rows, :]], axis=1)
 
     def mean_of(a, m):
         total = br[a, 0, m]
@@ -326,54 +376,61 @@
             total = total + br[a, j, m]
         return total * (1.0 / width)
 
-    def finish_back(m):
+    def finish_back(j):
+        m, v = chain_of(j), order[j]
         l1 = lax.rem(m + 1, n)
         late, early = inv[2, m], inv[1, m]
         c = late * late * mean_of(0, m)
         mean = mean_of(1, m) - c * mean_of(2, m)
-        for b in range(blocks):
-            at = slice(b * LANES, (b + 1) * LANES)
-            rows = slice(b * brow, (b + 1) * brow)
-            g = (wide[m, at, :] - c * xs[2, m, at, :].astype(F32)).astype(BF16)
-            grads[1, m, at, :] = g
-            d = (e1[m, rows, :] - c * e2[m, rows, :]).astype(BF16)
-            ds[1, m, rows, :] = d
-            u = xs[1, m, at, :].astype(F32) * early
-            g = g.astype(F32) + early * (gt[l1, at, :] * nn(kdt[l1, b], d) - u * mean)
-            g = g.astype(BF16)
-            grads[0, m, at, :] = g
-            p = probs[0, m, rows, :].reshape(per, src, tok)
-            ds[0, m, rows, :] = softmax_back(p, nn(vd[m, b], g)).astype(BF16)
-
+        for group in singles:
+            gs = []
+            for b in group:
+                at, rows = span(b)
+                g = (wide[v, at, :] - c * xs[2, m, at, :].astype(F32)).astype(BF16)
+                grads[1, v, at, :] = g
+                d = (e1[v, rows, :] - c * e2[m, rows, :]).astype(BF16)
+                ds[1, v, rows, :] = d
+                u = xs[1, m, at, :].astype(F32) * early
+                g = g.astype(F32) + early * (gt[l1, at, :] * nn(kdt[l1, b], d) - u * mean)
+                g = g.astype(BF16)
+                grads[0, v, at, :] = g
+                gs.append(g)
+            for b, dprob in zip(group, products(vd, m, group, gs)):
+                _, rows = span(b)
+                p = probs[0, m, rows, :].reshape(per, src, tok)
+                ds[0, v, rows, :] = softmax_back(p, dprob).astype(BF16)
+
+    keep([start_back(j) for j in range(n // 2)])
+    for lo, hi in [(j, j + 2) for j in range(n // 2, n - 2, 2)] + [(n - 2, n - 1), (n - 1, n)]:
+        for j in range(lo, hi):
+            arrive_c(j)
+        turned = [turn_c(j) for j in range(lo, hi)]
+        keep([start_back(j, turned[j - lo]) for j in range(lo, hi)])
+    peers(lambda p: br_copy(p, me).start())
+    for l in range(n):
+        ktot[l] = steps(of_spot(ds), of_chain(qs), l)
+    for l in range(n):
+        vtot[l] = steps(of_chain(plow), of_spot(grads), l)
+    peers(lambda p: br_copy(p, p).wait_recv())
     for j in range(n):
-        p = partners[j]
-        if j == 0:
-            own[2].wait()
-        else:
-            arrive_c(p)
-        m = lax.rem(p + n - TICKS % n, n)
-        turn_c(m)
-        start_back(m)
-    peers(lambda p: br_copy(p, me).start())
-    each(lambda m: key_step(2, m))
-    each(lambda m: value_step(2, m))
-    peers(lambda p: br_copy(p, p).wait_recv())
-    each(finish_back)
+        finish_back(j)
 
     def last(l):
-        steps = ktot[l] + paired(ds, qs, l)
-        kout_ref[l] = steps.astype(BF16)
-        gsend[l] = jnp.sum(steps * k_ref[l].astype(F32), axis=0, keepdims=True) / gin[l]
-
-    each(last)
+        total = ktot[l] + steps(pair_of_spot(ds), pair_of_chain(qs), l)
+        kout_ref[l] = total.astype(BF16)
+        gsend[l] = jnp.sum(total * k_ref[l].astype(F32), axis=0, keepdims=True) / gin[l]
+
+    for l in range(n):
+        last(l)
     own_gain = pltpu.make_async_copy(gsend.at[me], gdp.at[doc, me], dp_recv)
     others(lambda q, p: dp_copy(q, p, doc, me).start())
     own_gain.start()
 
     def finish(l):
-        vout_ref[l] = (vtot[l] + paired(plow, grads, l)).astype(BF16)
-
-    each(finish)
+        vout_ref[l] = (vtot[l] + steps(pair_of_chain(plow), pair_of_spot(grads), l)).astype(BF16)
+
+    for l in range(n):
+        finish(l)
 
     def drain(p):
         x_copy(p, me).wait_send()

time: 49.8 us -> 47 us (0.944)
  Pallas kernels: 49 us -> 46.2 us
    pallas_call x1, Pallas kernels: 48.3 us -> 45.4 us  [on_device(): pl.pallas_call(functools.partial(kernel, n, ndp, unroll), out_shape=(vmem...]
where the time goes in v4:
time: 47 us; the launch traced here: 46.8 us
  Pallas kernels  46.2 us (98%)
  between operations  0.64 us (1%)
    pallas_call x1, Pallas kernels, on_device(): pl.pallas_call(functools.partial(kernel, n, ndp, unroll), out_shape=(vmem...  45.4 us

profile of v4, /device:TPU:0, one launch (start us, length us, event | category | flops | bytes accessed | tf_op | source)
XLA Modules:
  0.0 46.8 jit_solution(8641869320616639861)
XLA Ops:
  0.6 45.4 %shard_map.76 = (bf16[8,24,512]{2,1,0:T(8,128)(2,1)S(1)}, bf16[8,24,512]{2,1,0:T(8,128)(2,1)S(1)}, f32[1,4096]{1,0:T(1,128)S(1)}) custom-call(bf16[128,4096]{1,0:T(8,128)(2,1)} %bitcast.4, bf16[128,4096]{1,0:T(8,128)(2,1)} %bitcast.5, bf16[8,24,512]{2,1,0:T(8,128)(2,1)} %bitcast.6, bf16[8,24,512]{2,1,0:T(8,128)(2,1)} %bitcast.7, f32[1,4096]{1,0:T(1,128)} %g_ref.1), custom_call_target="tpu_custom_call" | custom-call | tf_op jit(solution)/shard_map/pallas_call | solution.py:503
  46.1 0.8 %shard_map.77 = (bf16[1,8,24,512]{3,2,1,0:T(8,128)(2,1)}, bf16[1,8,24,512]{3,2,1,0:T(8,128)(2,1)}, f32[1,4096]{1,0:T(1,128)}) custom-call(bf16[8,24,512]{2,1,0:T(8,128)(2,1)S(1)} %get-tuple-element.6.keys, bf16[8,24,512]{2,1,0:T(8,128)(2,1)S(1)} %get-tuple-element.7.values, f32[1,4096]{1,0:T(1,128)S(1)} %get-tuple-element.8.gains), custom_call_target="tpu_custom_call" | custom-call | tf_op jit(solution)/shard_map/pallas_call | solution.py:516

commit v5 on v4

--- a/solution.py
+++ b/solution.py
@@ -29,7 +29,7 @@
     kout_ref, vout_ref, gout_ref,
     x_own, k_ref, v_ref,
     xin, cin, gin, stat, kd, vd, kdt, vdt, gt, xs, qs, probs, plow, raws, ds, grads,
-    wide, e1, e2, inv, ar, br, ktot, vtot, gsend, gdp,
+    wide, e1, e2, a1, a2, d1, d2, d3, ce, inv, ar, br, ktot, gsend, gdp,
     x_send, x_recv, c_send, c_recv, g_send, g_recv, st_send, st_recv,
     ar_send, ar_recv, br_send, br_recv, dp_send, dp_recv, loc,
 ):
@@ -165,7 +165,7 @@
     stat[me] = jnp.sum(total.T, axis=0, keepdims=True)
     peers(lambda p: st_copy(p, me).start())
     peers(lambda p: x_copy(p, me).start(), n // 2)
-    first_cut, second_cut = n - 2, n + 2
+    first_cut, second_cut = n - 2, n + 3
     c_send_units(0, first_cut)
     own[4].wait()
     own[5].wait()
@@ -233,15 +233,32 @@
         if more:
             ar[k, me, m] = sums
 
+    def response_0(m):
+        for group in groups:
+            out = products(vd, m, group, [xs[1, m, span(b)[0], :] for b in group])
+            for b, dprob in zip(group, out):
+                _, rows = span(b)
+                p = probs[0, m, rows, :].reshape(per, src, tok)
+                d3[m, rows, :] = softmax_back(p, dprob)
+
     def response(m):
+        l1 = lax.rem(m + 1, n)
+        early = inv[1, m]
         sums = jnp.zeros((1, tok), F32)
         for group in groups:
-            out = products(vd, lax.rem(m + 1, n), group, [xs[2, m, span(b)[0], :] for b in group])
-            for b, dprob in zip(group, out):
-                _, rows = span(b)
+            states = [xs[2, m, span(b)[0], :] for b in group]
+            hs = []
+            for b, x, dprob in zip(group, states, products(vd, l1, group, states)):
+                at, rows = span(b)
                 e = softmax_back(probs[1, m, rows, :].reshape(per, src, tok), dprob)
                 e2[m, rows, :] = e
                 sums = sums + jnp.sum(e * raws[1, m, rows, :], axis=0, keepdims=True)
+                a = gt[l1, at, :] * nn(kdt[l1, b], e.astype(BF16))
+                a2[m, at, :] = a
+                hs.append((x.astype(F32) + early * a).astype(BF16))
+            for b, dprob in zip(group, products(vd, m, group, hs)):
+                _, rows = span(b)
+                d2[m, rows, :] = softmax_back(probs[0, m, rows, :].reshape(per, src, tok), dprob)
         br[2, me, m] = sums
 
     def reduced(a, h):
@@ -294,6 +311,7 @@
     share(0, 1)
     c_send_units(first_cut, second_cut)
     turn_early(0, n // 4)
+    each(response_0)
     for k in range(1, TICKS):
         for h, (lo, hi) in enumerate(halves):
             inv[k, lo:hi] = lax.rsqrt(reduced(k - 1, h) + 1e-6)
@@ -376,29 +394,40 @@
             total = total + br[a, j, m]
         return total * (1.0 / width)
 
+    def advance(j):
+        m, v = chain_of(j), order[j]
+        l1 = lax.rem(m + 1, n)
+        early = inv[1, m]
+        for group in groups:
+            hs = []
+            for b in group:
+                at, rows = span(b)
+                a = gt[l1, at, :] * nn(kdt[l1, b], e1[v, rows, :].astype(BF16))
+                a1[v, at, :] = a
+                hs.append((wide[v, at, :] + early * a).astype(BF16))
+            for b, dprob in zip(group, products(vd, m, group, hs)):
+                _, rows = span(b)
+                d1[v, rows, :] = softmax_back(probs[0, m, rows, :].reshape(per, src, tok), dprob)
+
     def finish_back(j):
         m, v = chain_of(j), order[j]
-        l1 = lax.rem(m + 1, n)
         late, early = inv[2, m], inv[1, m]
         c = late * late * mean_of(0, m)
-        mean = mean_of(1, m) - c * mean_of(2, m)
-        for group in singles:
-            gs = []
-            for b in group:
-                at, rows = span(b)
-                g = (wide[v, at, :] - c * xs[2, m, at, :].astype(F32)).astype(BF16)
-                grads[1, v, at, :] = g
-                d = (e1[v, rows, :] - c * e2[m, rows, :]).astype(BF16)
-                ds[1, v, rows, :] = d
-                u = xs[1, m, at, :].astype(F32) * early
-                g = g.astype(F32) + early * (gt[l1, at, :] * nn(kdt[l1, b], d) - u * mean)
-                g = g.astype(BF16)
-                grads[0, v, at, :] = g
-                gs.append(g)
-            for b, dprob in zip(group, products(vd, m, group, gs)):
-                _, rows = span(b)
-                p = probs[0, m, rows, :].reshape(per, src, tok)
-                ds[0, v, rows, :] = softmax_back(p, dprob).astype(BF16)
+        e = early * early * (mean_of(1, m) - c * mean_of(2, m))
+        ce[0, v] = c
+        ce[1, v] = e
+        ds[1, v] = (e1[v] - c * e2[m]).astype(BF16)
+        ds[0, v] = (d1[v] - c * d2[m] - e * d3[m]).astype(BF16)
+
+    def gradients(j):
+        m, v = chain_of(j), order[j]
+        early, c, e = inv[1, m], ce[0, v], ce[1, v]
+        for b in range(blocks):
+            at, _ = span(b)
+            g = (wide[v, at, :] - c * xs[2, m, at, :].astype(F32)).astype(BF16)
+            grads[1, v, at, :] = g
+            step = early * (a1[v, at, :] - c * a2[m, at, :]) - e * xs[1, m, at, :].astype(F32)
+            grads[0, v, at, :] = (g.astype(F32) + step).astype(BF16)
 
     keep([start_back(j) for j in range(n // 2)])
     for lo, hi in [(j, j + 2) for j in range(n // 2, n - 2, 2)] + [(n - 2, n - 1), (n - 1, n)]:
@@ -409,8 +438,8 @@
     peers(lambda p: br_copy(p, me).start())
     for l in range(n):
         ktot[l] = steps(of_spot(ds), of_chain(qs), l)
-    for l in range(n):
-        vtot[l] = steps(of_chain(plow), of_spot(grads), l)
+    for j in range(n):
+        advance(j)
     peers(lambda p: br_copy(p, p).wait_recv())
     for j in range(n):
         finish_back(j)
@@ -427,8 +456,12 @@
     own_gain.start()
 
     def finish(l):
-        vout_ref[l] = (vtot[l] + steps(pair_of_chain(plow), pair_of_spot(grads), l)).astype(BF16)
-
+        total = steps(of_chain(plow), of_spot(grads), l)
+        total = total + steps(pair_of_chain(plow), pair_of_spot(grads), l)
+        vout_ref[l] = total.astype(BF16)
+
+    for j in range(n):
+        gradients(j)
     for l in range(n):
         finish(l)
 
@@ -490,9 +523,12 @@
         vmem((TICKS, n, rows, tok), F32),
         vmem((TICKS, n, rows, tok), BF16), vmem((TICKS, n, cols, tok), BF16),
         vmem((n, cols, tok), F32), vmem((n, rows, tok), F32), vmem((n, rows, tok), F32),
+        vmem((n, cols, tok), F32), vmem((n, cols, tok), F32),
+        vmem((n, rows, tok), F32), vmem((n, rows, tok), F32), vmem((n, rows, tok), F32),
+        vmem((2, n, 1, tok), F32),
         vmem((TICKS, n, 1, tok), F32),
         vmem((rounds, n, n, 1, tok), F32), vmem((3, n, n, 1, tok), F32),
-        vmem((n, src, cols), F32), vmem((n, src, cols), F32),
+        vmem((n, src, cols), F32),
         vmem((n, 1, cols), F32), vmem((ndp, n, 1, cols), F32),
         sem((n,)), sem((n,)), sem((2, n)), sem((2, n)), sem((n,)), sem((n,)), sem((n,)), sem((n,)),
         sem((rounds, 2, n)), sem((rounds, 2, n)), sem((n,)), sem((n,)), sem(()), sem(()), sem((6,)),

time: 47 us -> 45.5 us (0.968)
  Pallas kernels: 46.2 us -> 44.7 us
    pallas_call x1, Pallas kernels: 45.4 us -> 44 us  [on_device(): pl.pallas_call(functools.partial(kernel, n, ndp, unroll), out_shape=(vmem...]
where the time goes in v5:
time: 45.5 us; the launch traced here: 45.4 us
  Pallas kernels  44.7 us (98%)
  between operations  0.64 us (1%)
    pallas_call x1, Pallas kernels, on_device(): pl.pallas_call(functools.partial(kernel, n, ndp, unroll), out_shape=(vmem...  44 us

profile of v5, /device:TPU:0, one launch (start us, length us, event | category | flops | bytes accessed | tf_op | source)
XLA Modules:
  0.0 45.4 jit_solution(8722337096566275582)
XLA Ops:
  0.6 44.0 %shard_map.76 = (bf16[8,24,512]{2,1,0:T(8,128)(2,1)S(1)}, bf16[8,24,512]{2,1,0:T(8,128)(2,1)S(1)}, f32[1,4096]{1,0:T(1,128)S(1)}) custom-call(bf16[128,4096]{1,0:T(8,128)(2,1)} %bitcast.4, bf16[128,4096]{1,0:T(8,128)(2,1)} %bitcast.5, bf16[8,24,512]{2,1,0:T(8,128)(2,1)} %bitcast.6, bf16[8,24,512]{2,1,0:T(8,128)(2,1)} %bitcast.7, f32[1,4096]{1,0:T(1,128)} %g_ref.1), custom_call_target="tpu_custom_call" | custom-call | tf_op jit(solution)/shard_map/pallas_call | solution.py:539
  44.6 0.8 %shard_map.77 = (bf16[1,8,24,512]{3,2,1,0:T(8,128)(2,1)}, bf16[1,8,24,512]{3,2,1,0:T(8,128)(2,1)}, f32[1,4096]{1,0:T(1,128)}) custom-call(bf16[8,24,512]{2,1,0:T(8,128)(2,1)S(1)} %get-tuple-element.6.keys, bf16[8,24,512]{2,1,0:T(8,128)(2,1)S(1)} %get-tuple-element.7.values, f32[1,4096]{1,0:T(1,128)S(1)} %get-tuple-element.8.gains), custom_call_target="tpu_custom_call" | custom-call | tf_op jit(solution)/shard_map/pallas_call | solution.py:552

commit v6 on v5

--- a/solution.py
+++ b/solution.py
@@ -89,12 +89,19 @@
             src_ref=source, dst_ref=target, send_sem=send, recv_sem=recv,
             device_id={"section": p}, device_id_type=MESH)
 
+    def documents(body):
+        def step(d, c):
+            body(lax.rem(doc + d, ndp))
+            return c
+        lax.fori_loop(1, ndp, step, 0, unroll=ndp - 1 if ndp <= 4 else 1)
+
     def others(body):
-        def step(j, c):
-            place = lax.rem(doc * n + me + j, n * ndp)
-            body(lax.div(place, n), lax.rem(place, n))
-            return c
-        lax.fori_loop(1, n * ndp, step, 0)
+        def elsewhere(q):
+            for p in range(n):
+                body(q, p)
+        documents(elsewhere)
+        for p in partners[1:]:
+            body(doc, p)
 
     def cut(ref, p):
         return ref.at[:, pl.ds(pl.multiple_of(p * cols, LANES), cols)]

time: 45.5 us -> 45 us (0.989)
  Pallas kernels: 44.7 us -> 44.2 us
    pallas_call x1, Pallas kernels: 44 us -> 43.4 us  [on_device(): pl.pallas_call(functools.partial(kernel, n, ndp, unroll), out_shape=(vmem...]
where the time goes in v6:
time: 45 us; the launch traced here: 44.8 us
  Pallas kernels  44.2 us (98%)
  between operations  0.64 us (1%)
    pallas_call x1, Pallas kernels, on_device(): pl.pallas_call(functools.partial(kernel, n, ndp, unroll), out_shape=(vmem...  43.4 us

profile of v6, /device:TPU:0, one launch (start us, length us, event | category | flops | bytes accessed | tf_op | source)
XLA Modules:
  0.0 44.8 jit_solution(10207677787467385624)
XLA Ops:
  0.6 43.4 %shard_map.76 = (bf16[8,24,512]{2,1,0:T(8,128)(2,1)S(1)}, bf16[8,24,512]{2,1,0:T(8,128)(2,1)S(1)}, f32[1,4096]{1,0:T(1,128)S(1)}) custom-call(bf16[128,4096]{1,0:T(8,128)(2,1)} %bitcast.4, bf16[128,4096]{1,0:T(8,128)(2,1)} %bitcast.5, bf16[8,24,512]{2,1,0:T(8,128)(2,1)} %bitcast.6, bf16[8,24,512]{2,1,0:T(8,128)(2,1)} %bitcast.7, f32[1,4096]{1,0:T(1,128)} %g_ref.1), custom_call_target="tpu_custom_call" | custom-call | tf_op jit(solution)/shard_map/pallas_call | solution.py:546
  44.1 0.8 %shard_map.77 = (bf16[1,8,24,512]{3,2,1,0:T(8,128)(2,1)}, bf16[1,8,24,512]{3,2,1,0:T(8,128)(2,1)}, f32[1,4096]{1,0:T(1,128)}) custom-call(bf16[8,24,512]{2,1,0:T(8,128)(2,1)S(1)} %get-tuple-element.6.keys, bf16[8,24,512]{2,1,0:T(8,128)(2,1)S(1)} %get-tuple-element.7.values, f32[1,4096]{1,0:T(1,128)S(1)} %get-tuple-element.8.gains), custom_call_target="tpu_custom_call" | custom-call | tf_op jit(solution)/shard_map/pallas_call | solution.py:559
